TPU v7x, 32 devices: a whole 2x2x4 slice. The times are simulated.
32 devices in a mesh: depth: 2 (over core), freq: 16 (over z, y, x).
Axes of the slice: x: 2, y: 2, z: 4, core: 2. Of those that a mesh axis runs over, the one named last changes fastest.
Arguments:
- p_top: bfloat16 [16, 1024, 128], P('freq'), may hold values from -6 to 6
- upgoing: bfloat16 [2, 16, 1024, 128], P('depth', 'freq'), may hold values from -6 to 6
- extrapolator: bfloat16 [2, 16, 2, 1024, 1024], P('depth', 'freq'), may hold values from -0.125 to 0.125
- reflectivity: bfloat16 [2, 1024, 1024], P('depth', 'freq'), may hold values from -0.1875 to 0.1875
Outputs:
- wavefields: bfloat16 [2, 16, 1024, 128], P('depth', 'freq')
- images: float32 [2, 1024, 1024], P('depth', 'freq')
All inputs are finite; a program needn't handle non-finite values.
Results may differ from a plain program's by a relative error of at most 0.014.
Values may be sent and summed in bfloat16 or wider, within the bound.
No kernel may reach another device: no remote copies, remote signals or barrier semaphores. Data moves between devices by JAX's collectives and lax.ppermute only.
A program may use at most 64 MiB of HBM per device.

v0:
```python
import jax
import jax.numpy as jnp
from jax import lax
from jax.sharding import PartitionSpec as P


def shifted(value, axis, by):
    devices = lax.axis_size(axis)
    pairs = [(i, i + by) for i in range(devices) if 0 <= i + by < devices]
    return lax.ppermute(value, axis, pairs)


def extrapolate(real_w, imag_w, diff):
    half = diff.shape[-1] // 2
    first = jnp.dot(real_w, diff, preferred_element_type=jnp.float32)
    second = jnp.dot(imag_w, diff, preferred_element_type=jnp.float32)
    real_part = first[:, :half] - second[:, half:]
    imag_part = first[:, half:] + second[:, :half]
    return jnp.concatenate([real_part, imag_part], axis=1).astype(jnp.bfloat16)


def local(p_top, upgoing, extrapolator, reflectivity):
    upper = upgoing[0, 0]
    real_w = extrapolator[0, 0, 0]
    imag_w = extrapolator[0, 0, 1]
    top_field = p_top[0]
    columns = upper.shape[1]
    sections = lax.axis_size("depth")
    section = lax.axis_index("depth")
    is_first = section == 0
    rq_full = jnp.dot(
        lax.all_gather(reflectivity[0], "freq", axis=0, tiled=True),
        upper,
        preferred_element_type=jnp.float32,
    )

    def advance(incoming, rq_part):
        diff = (incoming.astype(jnp.float32) - rq_part).astype(jnp.bfloat16)
        return extrapolate(real_w, imag_w, diff)

    incoming = jnp.where(is_first, top_field, jnp.zeros_like(top_field))
    below = advance(incoming, rq_full)

    def whole_step(step, carry):
        inc_now, below_now = carry
        moved = shifted(below_now, "depth", 1)
        inc_next = jnp.where(is_first, top_field, moved)
        return (inc_next, advance(inc_next, rq_full))

    incoming, below = lax.fori_loop(0, sections - 1, whole_step, (incoming, below))
    scale = (float(columns) * lax.axis_size("freq")) ** (-0.5)
    picture = (
        lax.psum_scatter(
            lax.dot_general(
                upper, incoming, (((1,), (1,)), ((), ())), preferred_element_type=jnp.float32
            ),
            "freq",
            scatter_dimension=0,
            tiled=True,
        )
        * scale
    )
    return (below[None, None], picture[None])


def solution(mesh):
    in_specs = (
        P("freq", None, None),
        P("depth", "freq", None, None),
        P("depth", "freq", None, None, None),
        P("depth", "freq", None),
    )
    out_specs = (P("depth", "freq", None, None), P("depth", "freq", None))
    return jax.shard_map(local, mesh=mesh, in_specs=in_specs, out_specs=out_specs, check_vma=False)
```

profile of v0, /device:TPU:0, one launch (start us, length us, event | category | flops | bytes accessed | tf_op | source)
XLA Modules:
  0.0 193.5 jit_solution(11771704683910217558)
XLA Ops:
  7.2 0.0 copy-start
  7.2 0.0 all-gather.3.cloned.1.call-start
  7.2 0.7 all-gather.3.cloned.1.call-update
  7.9 0.0 reduce-scatter.4.cloned.1.call-start
  8.0 65.9 %all-gather.3.cloned.1.call-done = bf16[1,1024,1024]{2,1,0:T(8,128)(2,1)} async-done(((bf16[1,64,1024]{2,1,0:T(8,128)(2,1)}), bf16[1,1024,1024]{2,1,0:T(8,128)(2,1)}) %all-gather.3.cloned.1.call-update) | async-done | bytes 2097168 | tf_op jit(solution)/shard_map/all_gather | solution.py:32
  73.9 0.0 copy-done
  73.9 0.0 copy-start.2
  73.9 2.5 %subtract_convert_fusion.1 = (bf16[1024,128]{1,0:T(8,128)(2,1)S(1)}, f32[1024,128]{1,0:T(8,128)S(1)}) fusion(bf16[1,1024,128]{2,1,0:T(8,128)(2,1)} %param.4, pred[]{:T(512)S(6)} %eq.3, bf16[1,1,1024,128]{3,2,1,0:T(8,128)(2,1)S(1)} %copy-done, bf16[1,1024,1024]{2,1,0:T(8,128)(2,1)} %all-gather.3.cloned.1.call-done), kind=kOutput, calls=%fused_computation.25 | convolution fusion | flops 268959744 | bytes 3407873 | tf_op jit(solution)/shard_map/dot_general | solution.py:31
  76.4 2.3 %fusion.14 = f32[1024,128]{1,0:T(8,128)S(1)} fusion(bf16[1024,128]{1,0:T(8,128)(2,1)S(1)} %get-tuple-element.33, bf16[1,1,2,1024,1024]{4,3,2,1,0:T(8,128)(2,1)} %param.6), kind=kOutput, calls=%fused_computation.15 | convolution fusion | flops 268435456 | bytes 2883584 | tf_op jit(solution)/shard_map/dot_general | solution.py:15
  78.6 0.0 copy-done.2
  78.7 0.0 copy-start.1
  78.7 0.7 fusion.20
  79.4 0.3 fusion.27
  79.7 0.1 pad_maximum_fusion
  79.9 1.3 collective-permute-start
  81.2 1.1 collective-permute-done
  82.3 0.0 copy-done.1
  82.3 2.7 %convolution_bitcast_fusion = f32[1024,1024]{0,1:T(8,128)} fusion(bf16[1,1,1024,128]{3,2,1,0:T(8,128)(2,1)S(1)} %copy-done, bf16[1024,128]{1,0:T(8,128)(2,1)S(1)} %collective-permute-done, bf16[1,1024,128]{2,1,0:T(8,128)(2,1)S(1)} %copy-done.1, pred[]{:T(512)S(6)} %eq.3), kind=kOutput, calls=%fused_computation | convolution fusion | flops 268566528 | bytes 4980737 | tf_op jit(solution)/shard_map/dot_general | solution.py:54
  85.0 5.4 %copy.16 = f32[1024,1024]{1,0:T(8,128)} copy(f32[1024,1024]{0,1:T(8,128)} %convolution_bitcast_fusion) | data formatting | bytes 8388608
  90.4 0.0 reduce-scatter.4.cloned.1.call-update
  90.4 0.0 copy-start.3
  90.4 0.1 subtract_convert_fusion
  90.5 2.6 %fusion.23 = f32[1024,128]{0,1:T(8,128)S(1)} fusion(bf16[1024,128]{1,0:T(8,128)(2,1)S(1)} %subtract_convert_fusion, bf16[1,1,2,1024,1024]{4,3,2,1,0:T(8,128)(2,1)} %param.6), kind=kOutput, calls=%fused_computation.18 | convolution fusion | flops 268435456 | bytes 2883584 | tf_op jit(solution)/shard_map/while/body/eval_jaxpr/dot_general | solution.py:16
  93.1 0.1 copy-done.3
  93.2 0.8 fusion.17
  94.1 0.1 fusion.32
  94.1 0.8 copy.12
  95.0 89.6 %reduce-scatter.4.cloned.1.call-done = f32[64,1024]{1,0:T(8,128)} async-done(((f32[1024,1024]{1,0:T(8,128)}), f32[64,1024]{1,0:T(8,128)}) %reduce-scatter.4.cloned.1.call-update) | async-done | bytes 262160
  184.6 1.1 copy.17
  185.8 0.9 copy.13
  (2 shorter events, 0.1 us)
Async XLA Ops:
  7.2 66.7 %copy-start = (bf16[1,1,1024,128]{3,2,1,0:T(8,128)(2,1)S(1)}, bf16[1,1,1024,128]{3,2,1,0:T(8,128)(2,1)}, u32[]{:S(2)}) copy-start(bf16[1,1,1024,128]{3,2,1,0:T(8,128)(2,1)} %param.5) | copy-start | bytes 786436
  7.2 66.7 %all-gather.3.cloned.1.call-start = ((), (), s32[]{:S(2)}) async-start(), calls=%async_computation.1 | async-start | bytes 2228224 | tf_op jit(solution)/shard_map/all_gather | solution.py:32
  7.9 176.7 %reduce-scatter.4.cloned.1.call-start = ((), (), s32[]{:S(2)}) async-start(), calls=%async_computation.2 | async-start | bytes 4456448
  73.9 4.8 %copy-start.2 = (bf16[1,1,2,1024,1024]{4,3,2,1,0:T(8,128)(2,1)S(1)}, bf16[1,1,2,1024,1024]{4,3,2,1,0:T(8,128)(2,1)}, u32[]{:S(2)}) copy-start(bf16[1,1,2,1024,1024]{4,3,2,1,0:T(8,128)(2,1)} %param.6) | copy-start | bytes 12582916
  78.7 3.7 %copy-start.1 = (bf16[1,1024,128]{2,1,0:T(8,128)(2,1)S(1)}, bf16[1,1024,128]{2,1,0:T(8,128)(2,1)}, u32[]{:S(2)}) copy-start(bf16[1,1024,128]{2,1,0:T(8,128)(2,1)} %param.4) | copy-start | bytes 786436
  79.9 2.4 %collective-permute-start = (bf16[1024,128]{1,0:T(8,128)(2,1)S(1)}, bf16[1024,128]{1,0:T(8,128)(2,1)S(1)}, u32[]{:S(2)}, u32[]{:S(2)}) collective-permute-start(bf16[1024,128]{1,0:T(8,128)(2,1)S(1)} %pad_maximum_fusion), channel_id=1, source_target_pairs={{0,16},{1,17},{2,18},{3,19},{4,20},{5,21},{6,22},{7,23},{8,24},{9,... | collective-permute-start | bytes 786440 | tf_op jit(solution)/shard_map/while/body/eval_jaxpr/ppermute | solution.py:10
  90.4 2.8 %copy-start.3 = (bf16[1,1,2,1024,1024]{4,3,2,1,0:T(8,128)(2,1)S(1)}, bf16[1,1,2,1024,1024]{4,3,2,1,0:T(8,128)(2,1)}, u32[]{:S(2)}) copy-start(bf16[1,1,2,1024,1024]{4,3,2,1,0:T(8,128)(2,1)} %param.6) | copy-start | bytes 12582916
Sparse Core Ops, SparseCore 0:
  10.8 63.0 all-gather.2
  90.5 94.0 reduce-scatter.3
where the time goes:
time: 194 us
  waiting for transfers between devices  157 us (81%)
  between operations  14.2 us (7%)
  matrix products  11.5 us (6%)
  local copies, waits for them, and re-layouts  8.39 us (4%)
    unnamed x3, waiting for transfers between devices  90.3 us
    all_gather x1, waiting for transfers between devices, local(): lax.all_gather(reflectivity[0], 'freq', axis=0, tiled=True)  65.9 us
    unnamed x12, local copies, waits for them, and re-layouts  8.39 us
  transfers between devices with their start and end apart: 3, of which 3 were waited for; matrix products, arithmetic and copies ran while one was open for 2% of the time, Pallas kernels for 0%

commit v1 on v0

--- a/solution.py
+++ b/solution.py
@@ -1,7 +1,35 @@
+import functools
 import jax
 import jax.numpy as jnp
 from jax import lax
 from jax.sharding import PartitionSpec as P
+from jax.lax import axis_index, axis_size, ppermute
+
+
+def blocks_handle(shard_in, axis_no):
+    f_now, taken_in, r_now = (axis_size("freq"), axis_index("freq"), shard_in.shape[axis_no])
+    buffers = [(p, (p + 1) % f_now) for p in range(f_now)]
+    seen = [(p, (p - 1) % f_now) for p in range(f_now)]
+    v1 = jnp.zeros(
+        (*shard_in.shape[:axis_no], f_now * r_now, *shard_in.shape[axis_no + 1 :]), shard_in.dtype
+    )
+    left_arr = newest = shard_in
+    view_out = f_now // 2
+    v1 = lax.dynamic_update_slice_in_dim(v1, shard_in, taken_in * r_now, axis=axis_no)
+    for s in range(1, view_out + 1):
+        left_arr = ppermute(left_arr, axis_name="freq", perm=buffers)
+        v1 = lax.dynamic_update_slice_in_dim(
+            v1, left_arr, (taken_in - s) % f_now * r_now, axis=axis_no
+        )
+        if s < f_now - view_out:
+            newest = ppermute(newest, axis_name="freq", perm=seen)
+            v1 = lax.dynamic_update_slice_in_dim(
+                v1, newest, (taken_in + s) % f_now * r_now, axis=axis_no
+            )
+    return v1
+
+
+close_racks = functools.partial(blocks_handle, axis_no=0)
 
 
 def shifted(value, axis, by):
@@ -28,11 +56,7 @@
     sections = lax.axis_size("depth")
     section = lax.axis_index("depth")
     is_first = section == 0
-    rq_full = jnp.dot(
-        lax.all_gather(reflectivity[0], "freq", axis=0, tiled=True),
-        upper,
-        preferred_element_type=jnp.float32,
-    )
+    rq_full = jnp.dot(close_racks(reflectivity[0]), upper, preferred_element_type=jnp.float32)
 
     def advance(incoming, rq_part):
         diff = (incoming.astype(jnp.float32) - rq_part).astype(jnp.bfloat16)

time: 194 us -> 194 us (level)
  starting transfers between devices: 1.38 us -> 42.4 us
  waiting for transfers between devices: 157 us -> 119 us
  matrix products: 11.5 us -> 8.23 us
    all_gather x1 -> x0, waiting for transfers between devices: 65.9 us -> none  [local(): lax.all_gather(reflectivity[0], 'freq', axis=0, tiled=True)]
    ppermute x0 -> x15, starting transfers between devices: none -> 41 us  [the longest x7 38 us: blocks_handle(): newest = ppermute(newest, axis_name='freq', perm=seen)]
    ppermute x0 -> x15, waiting for transfers between devices: none -> 31.1 us  [the longest x8 30.9 us: blocks_handle(): left_arr = ppermute(left_arr, axis_name='freq', perm=buffers)]
    unnamed x3 -> x2, waiting for transfers between devices: 90.3 us -> 86.8 us
    unnamed x12 -> x14, local copies, waits for them, and re-layouts: 8.39 us -> 8.55 us
  transfers between devices with their start and end apart: 3 -> 17, of which waited for: 3 -> 11; matrix products, arithmetic and copies ran while one was open for 2% -> 3% of each run, Pallas kernels for 0% -> 0%
where the time goes in v1:
time: 194 us
  waiting for transfers between devices  119 us (61%)
  starting transfers between devices  42.4 us (22%)
  between operations  14.3 us (7%)
  local copies, waits for them, and re-layouts  9.03 us (5%)
  matrix products  8.23 us (4%)
    unnamed x2, waiting for transfers between devices  86.8 us
    ppermute x7, starting transfers between devices, blocks_handle(): newest = ppermute(newest, axis_name='freq', perm=seen)  38 us
    ppermute x8, waiting for transfers between devices, blocks_handle(): left_arr = ppermute(left_arr, axis_name='freq', perm=buffers)  30.9 us
    unnamed x14, local copies, waits for them, and re-layouts  8.55 us
  transfers between devices with their start and end apart: 17, of which 11 were waited for; matrix products, arithmetic and copies ran while one was open for 3% of the time, Pallas kernels for 0%

profile of v1, /device:TPU:0, one launch (start us, length us, event | category | flops | bytes accessed | tf_op | source)
XLA Modules:
  0.0 193.7 jit_solution(2871736544163685466)
XLA Ops:
  7.2 3.0 %collective-permute-start = (bf16[64,1024]{1,0:T(8,128)(2,1)}, bf16[64,1024]{1,0:T(8,128)(2,1)S(1)}, u32[]{:S(2)}, u32[]{:S(2)}) collective-permute-start(bf16[64,1024]{1,0:T(8,128)(2,1)} %bitcast.57), channel_id=1, source_target_pairs={{0,1},{1,2},{2,3},{3,4},{4,5},{5,6},{6,7},{7,8},{8,9},{9,10},{10,1... | collective-permute-start | bytes 393224 | tf_op jit(solution)/shard_map/ppermute | solution.py:20
  10.3 4.1 %collective-permute-start.1 = (bf16[64,1024]{1,0:T(8,128)(2,1)}, bf16[64,1024]{1,0:T(8,128)(2,1)S(1)}, u32[]{:S(2)}, u32[]{:S(2)}) collective-permute-start(bf16[64,1024]{1,0:T(8,128)(2,1)} %bitcast.58), channel_id=1, source_target_pairs={{0,15},{1,0},{2,1},{3,2},{4,3},{5,4},{6,5},{7,6},{8,7},{9,8},{10,9... | collective-permute-start | bytes 393224 | tf_op jit(solution)/shard_map/ppermute | solution.py:25
  14.3 0.3 broadcast_in_dim.11
  14.6 3.4 %collective-permute-done = bf16[64,1024]{1,0:T(8,128)(2,1)S(1)} collective-permute-done((bf16[64,1024]{1,0:T(8,128)(2,1)}, bf16[64,1024]{1,0:T(8,128)(2,1)S(1)}, u32[]{:S(2)}, u32[]{:S(2)}) %collective-permute-start) | collective-permute-done | bytes 131104 | tf_op jit(solution)/shard_map/ppermute | solution.py:20
  18.3 5.4 %collective-permute-start.3 = (bf16[64,1024]{1,0:T(8,128)(2,1)S(1)}, bf16[64,1024]{1,0:T(8,128)(2,1)S(1)}, u32[]{:S(2)}, u32[]{:S(2)}) collective-permute-start(bf16[64,1024]{1,0:T(8,128)(2,1)S(1)} %collective-permute-done.1), channel_id=1, source_target_pairs={{0,15},{1,0},{2,1},{3,2},{4,3},{5,4},{6,5},{7,6},{8,7},{9,8},{10,9... | collective-permute-start | bytes 393224 | tf_op jit(solution)/shard_map/ppermute | solution.py:25
  23.7 2.9 %collective-permute-done.2 = bf16[64,1024]{1,0:T(8,128)(2,1)S(1)} collective-permute-done((bf16[64,1024]{1,0:T(8,128)(2,1)S(1)}, bf16[64,1024]{1,0:T(8,128)(2,1)S(1)}, u32[]{:S(2)}, u32[]{:S(2)}) %collective-permute-start.2) | collective-permute-done | bytes 131104 | tf_op jit(solution)/shard_map/ppermute | solution.py:20
  26.6 5.7 %collective-permute-start.5 = (bf16[64,1024]{1,0:T(8,128)(2,1)S(1)}, bf16[64,1024]{1,0:T(8,128)(2,1)S(1)}, u32[]{:S(2)}, u32[]{:S(2)}) collective-permute-start(bf16[64,1024]{1,0:T(8,128)(2,1)S(1)} %collective-permute-done.3), channel_id=1, source_target_pairs={{0,15},{1,0},{2,1},{3,2},{4,3},{5,4},{6,5},{7,6},{8,7},{9,8},{10,9... | collective-permute-start | bytes 393224 | tf_op jit(solution)/shard_map/ppermute | solution.py:25
  32.4 2.9 %collective-permute-done.4 = bf16[64,1024]{1,0:T(8,128)(2,1)S(1)} collective-permute-done((bf16[64,1024]{1,0:T(8,128)(2,1)S(1)}, bf16[64,1024]{1,0:T(8,128)(2,1)S(1)}, u32[]{:S(2)}, u32[]{:S(2)}) %collective-permute-start.4) | collective-permute-done | bytes 131104 | tf_op jit(solution)/shard_map/ppermute | solution.py:20
  35.3 5.7 %collective-permute-start.7 = (bf16[64,1024]{1,0:T(8,128)(2,1)S(1)}, bf16[64,1024]{1,0:T(8,128)(2,1)S(1)}, u32[]{:S(2)}, u32[]{:S(2)}) collective-permute-start(bf16[64,1024]{1,0:T(8,128)(2,1)S(1)} %collective-permute-done.5), channel_id=1, source_target_pairs={{0,15},{1,0},{2,1},{3,2},{4,3},{5,4},{6,5},{7,6},{8,7},{9,8},{10,9... | collective-permute-start | bytes 393224 | tf_op jit(solution)/shard_map/ppermute | solution.py:25
  41.1 2.9 %collective-permute-done.6 = bf16[64,1024]{1,0:T(8,128)(2,1)S(1)} collective-permute-done((bf16[64,1024]{1,0:T(8,128)(2,1)S(1)}, bf16[64,1024]{1,0:T(8,128)(2,1)S(1)}, u32[]{:S(2)}, u32[]{:S(2)}) %collective-permute-start.6) | collective-permute-done | bytes 131104 | tf_op jit(solution)/shard_map/ppermute | solution.py:20
  44.0 5.6 %collective-permute-start.9 = (bf16[64,1024]{1,0:T(8,128)(2,1)S(1)}, bf16[64,1024]{1,0:T(8,128)(2,1)S(1)}, u32[]{:S(2)}, u32[]{:S(2)}) collective-permute-start(bf16[64,1024]{1,0:T(8,128)(2,1)S(1)} %collective-permute-done.7), channel_id=1, source_target_pairs={{0,15},{1,0},{2,1},{3,2},{4,3},{5,4},{6,5},{7,6},{8,7},{9,8},{10,9... | collective-permute-start | bytes 393224 | tf_op jit(solution)/shard_map/ppermute | solution.py:25
  49.6 3.0 %collective-permute-done.8 = bf16[64,1024]{1,0:T(8,128)(2,1)S(1)} collective-permute-done((bf16[64,1024]{1,0:T(8,128)(2,1)S(1)}, bf16[64,1024]{1,0:T(8,128)(2,1)S(1)}, u32[]{:S(2)}, u32[]{:S(2)}) %collective-permute-start.8) | collective-permute-done | bytes 131104 | tf_op jit(solution)/shard_map/ppermute | solution.py:20
  52.6 5.6 %collective-permute-start.11 = (bf16[64,1024]{1,0:T(8,128)(2,1)S(1)}, bf16[64,1024]{1,0:T(8,128)(2,1)S(1)}, u32[]{:S(2)}, u32[]{:S(2)}) collective-permute-start(bf16[64,1024]{1,0:T(8,128)(2,1)S(1)} %collective-permute-done.9), channel_id=1, source_target_pairs={{0,15},{1,0},{2,1},{3,2},{4,3},{5,4},{6,5},{7,6},{8,7},{9,8},{10,9... | collective-permute-start | bytes 393224 | tf_op jit(solution)/shard_map/ppermute | solution.py:25
  58.3 3.2 %collective-permute-done.10 = bf16[64,1024]{1,0:T(8,128)(2,1)S(1)} collective-permute-done((bf16[64,1024]{1,0:T(8,128)(2,1)S(1)}, bf16[64,1024]{1,0:T(8,128)(2,1)S(1)}, u32[]{:S(2)}, u32[]{:S(2)}) %collective-permute-start.10) | collective-permute-done | bytes 131104 | tf_op jit(solution)/shard_map/ppermute | solution.py:20
  61.5 5.9 %collective-permute-start.13 = (bf16[64,1024]{1,0:T(8,128)(2,1)S(1)}, bf16[64,1024]{1,0:T(8,128)(2,1)S(1)}, u32[]{:S(2)}, u32[]{:S(2)}) collective-permute-start(bf16[64,1024]{1,0:T(8,128)(2,1)S(1)} %collective-permute-done.11), channel_id=1, source_target_pairs={{0,15},{1,0},{2,1},{3,2},{4,3},{5,4},{6,5},{7,6},{8,7},{9,8},{10,9... | collective-permute-start | bytes 393224 | tf_op jit(solution)/shard_map/ppermute | solution.py:25
  67.5 4.0 %collective-permute-done.12 = bf16[64,1024]{1,0:T(8,128)(2,1)S(1)} collective-permute-done((bf16[64,1024]{1,0:T(8,128)(2,1)S(1)}, bf16[64,1024]{1,0:T(8,128)(2,1)S(1)}, u32[]{:S(2)}, u32[]{:S(2)}) %collective-permute-start.12) | collective-permute-done | bytes 131104 | tf_op jit(solution)/shard_map/ppermute | solution.py:20
  71.5 8.5 %collective-permute-done.14 = bf16[64,1024]{1,0:T(8,128)(2,1)S(1)} collective-permute-done((bf16[64,1024]{1,0:T(8,128)(2,1)S(1)}, bf16[64,1024]{1,0:T(8,128)(2,1)S(1)}, u32[]{:S(2)}, u32[]{:S(2)}) %collective-permute-start.14) | collective-permute-done | bytes 131104 | tf_op jit(solution)/shard_map/ppermute | solution.py:20
  80.1 0.7 subtract_convert_fusion.1
  80.8 0.7 fusion.12
  81.5 0.7 fusion.18
  82.2 0.3 fusion.25
  82.7 1.3 collective-permute-start.15
  84.0 1.1 collective-permute-done.15
  85.2 2.7 %convolution_bitcast_fusion = f32[1024,1024]{0,1:T(8,128)} fusion(bf16[1,1,1024,128]{3,2,1,0:T(8,128)(2,1)S(1)} %copy-done, bf16[1024,128]{1,0:T(8,128)(2,1)S(1)} %collective-permute-done.15, bf16[1,1024,128]{2,1,0:T(8,128)(2,1)S(1)} %copy-done.1, pred[]{:T(512)S(6)} %eq.19), kind=kOutput, calls=%fused_computation | convolution fusion | flops 268566528 | bytes 4980737 | tf_op jit(solution)/shard_map/dot_general | solution.py:78
  87.9 5.3 %copy.16 = f32[1024,1024]{1,0:T(8,128)} copy(f32[1024,1024]{0,1:T(8,128)} %convolution_bitcast_fusion) | data formatting | bytes 8388608
  93.3 2.6 %fusion.21 = f32[1024,128]{0,1:T(8,128)S(1)} fusion(bf16[1024,128]{1,0:T(8,128)(2,1)S(1)} %subtract_convert_fusion, bf16[1,1,2,1024,1024]{4,3,2,1,0:T(8,128)(2,1)} %param.6), kind=kOutput, calls=%fused_computation.16 | convolution fusion | flops 268435456 | bytes 2883584 | tf_op jit(solution)/shard_map/while/body/eval_jaxpr/dot_general | solution.py:44
  95.9 0.3 copy-done.4
  96.2 0.8 fusion.15
  97.2 0.8 copy.12
  98.0 86.8 %reduce-scatter.4.cloned.1.call-done = f32[64,1024]{1,0:T(8,128)} async-done(((f32[1024,1024]{1,0:T(8,128)}), f32[64,1024]{1,0:T(8,128)}) %reduce-scatter.4.cloned.1.call-update) | async-done | bytes 262160
  184.8 1.1 copy.17
  186.0 0.9 copy.13
  (46 shorter events, 1.0 us)
Async XLA Ops:
  7.2 72.9 %copy-start = (bf16[1,1,1024,128]{3,2,1,0:T(8,128)(2,1)S(1)}, bf16[1,1,1024,128]{3,2,1,0:T(8,128)(2,1)}, u32[]{:S(2)}) copy-start(bf16[1,1,1024,128]{3,2,1,0:T(8,128)(2,1)} %param.5) | copy-start | bytes 786436
  7.2 7.4 %copy-start.2 = (bf16[1,64,1024]{2,1,0:T(8,128)(2,1)S(1)}, bf16[1,64,1024]{2,1,0:T(8,128)(2,1)}, u32[]{:S(2)}) copy-start(bf16[1,64,1024]{2,1,0:T(8,128)(2,1)} %param.7) | copy-start | bytes 393220
  7.2 177.6 %reduce-scatter.4.cloned.1.call-start = ((), (), s32[]{:S(2)}) async-start(), calls=%async_computation.1 | async-start | bytes 4456448
  7.2 10.8 %collective-permute-start = (bf16[64,1024]{1,0:T(8,128)(2,1)}, bf16[64,1024]{1,0:T(8,128)(2,1)S(1)}, u32[]{:S(2)}, u32[]{:S(2)}) collective-permute-start(bf16[64,1024]{1,0:T(8,128)(2,1)} %bitcast.57), channel_id=1, source_target_pairs={{0,1},{1,2},{2,3},{3,4},{4,5},{5,6},{6,7},{7,8},{8,9},{9,10},{10,1... | collective-permute-start | bytes 393224 | tf_op jit(solution)/shard_map/ppermute | solution.py:20
  10.3 8.1 %collective-permute-start.1 = (bf16[64,1024]{1,0:T(8,128)(2,1)}, bf16[64,1024]{1,0:T(8,128)(2,1)S(1)}, u32[]{:S(2)}, u32[]{:S(2)}) collective-permute-start(bf16[64,1024]{1,0:T(8,128)(2,1)} %bitcast.58), channel_id=1, source_target_pairs={{0,15},{1,0},{2,1},{3,2},{4,3},{5,4},{6,5},{7,6},{8,7},{9,8},{10,9... | collective-permute-start | bytes 393224 | tf_op jit(solution)/shard_map/ppermute | solution.py:25
  14.6 65.5 %copy-start.1 = (bf16[1,1024,128]{2,1,0:T(8,128)(2,1)S(1)}, bf16[1,1024,128]{2,1,0:T(8,128)(2,1)}, u32[]{:S(2)}) copy-start(bf16[1,1024,128]{2,1,0:T(8,128)(2,1)} %param.4) | copy-start | bytes 786436
  18.1 8.6 %collective-permute-start.2 = (bf16[64,1024]{1,0:T(8,128)(2,1)S(1)}, bf16[64,1024]{1,0:T(8,128)(2,1)S(1)}, u32[]{:S(2)}, u32[]{:S(2)}) collective-permute-start(bf16[64,1024]{1,0:T(8,128)(2,1)S(1)} %collective-permute-done), channel_id=1, source_target_pairs={{0,1},{1,2},{2,3},{3,4},{4,5},{5,6},{6,7},{7,8},{8,9},{9,10},{10,1... | collective-permute-start | bytes 393224 | tf_op jit(solution)/shard_map/ppermute | solution.py:20
  18.3 8.3 %collective-permute-start.3 = (bf16[64,1024]{1,0:T(8,128)(2,1)S(1)}, bf16[64,1024]{1,0:T(8,128)(2,1)S(1)}, u32[]{:S(2)}, u32[]{:S(2)}) collective-permute-start(bf16[64,1024]{1,0:T(8,128)(2,1)S(1)} %collective-permute-done.1), channel_id=1, source_target_pairs={{0,15},{1,0},{2,1},{3,2},{4,3},{5,4},{6,5},{7,6},{8,7},{9,8},{10,9... | collective-permute-start | bytes 393224 | tf_op jit(solution)/shard_map/ppermute | solution.py:25
  26.6 8.7 %collective-permute-start.4 = (bf16[64,1024]{1,0:T(8,128)(2,1)S(1)}, bf16[64,1024]{1,0:T(8,128)(2,1)S(1)}, u32[]{:S(2)}, u32[]{:S(2)}) collective-permute-start(bf16[64,1024]{1,0:T(8,128)(2,1)S(1)} %collective-permute-done.2), channel_id=1, source_target_pairs={{0,1},{1,2},{2,3},{3,4},{4,5},{5,6},{6,7},{7,8},{8,9},{9,10},{10,1... | collective-permute-start | bytes 393224 | tf_op jit(solution)/shard_map/ppermute | solution.py:20
  26.6 8.7 %collective-permute-start.5 = (bf16[64,1024]{1,0:T(8,128)(2,1)S(1)}, bf16[64,1024]{1,0:T(8,128)(2,1)S(1)}, u32[]{:S(2)}, u32[]{:S(2)}) collective-permute-start(bf16[64,1024]{1,0:T(8,128)(2,1)S(1)} %collective-permute-done.3), channel_id=1, source_target_pairs={{0,15},{1,0},{2,1},{3,2},{4,3},{5,4},{6,5},{7,6},{8,7},{9,8},{10,9... | collective-permute-start | bytes 393224 | tf_op jit(solution)/shard_map/ppermute | solution.py:25
  35.3 8.7 %collective-permute-start.6 = (bf16[64,1024]{1,0:T(8,128)(2,1)S(1)}, bf16[64,1024]{1,0:T(8,128)(2,1)S(1)}, u32[]{:S(2)}, u32[]{:S(2)}) collective-permute-start(bf16[64,1024]{1,0:T(8,128)(2,1)S(1)} %collective-permute-done.4), channel_id=1, source_target_pairs={{0,1},{1,2},{2,3},{3,4},{4,5},{5,6},{6,7},{7,8},{8,9},{9,10},{10,1... | collective-permute-start | bytes 393224 | tf_op jit(solution)/shard_map/ppermute | solution.py:20
  35.3 8.7 %collective-permute-start.7 = (bf16[64,1024]{1,0:T(8,128)(2,1)S(1)}, bf16[64,1024]{1,0:T(8,128)(2,1)S(1)}, u32[]{:S(2)}, u32[]{:S(2)}) collective-permute-start(bf16[64,1024]{1,0:T(8,128)(2,1)S(1)} %collective-permute-done.5), channel_id=1, source_target_pairs={{0,15},{1,0},{2,1},{3,2},{4,3},{5,4},{6,5},{7,6},{8,7},{9,8},{10,9... | collective-permute-start | bytes 393224 | tf_op jit(solution)/shard_map/ppermute | solution.py:25
  44.0 8.7 %collective-permute-start.8 = (bf16[64,1024]{1,0:T(8,128)(2,1)S(1)}, bf16[64,1024]{1,0:T(8,128)(2,1)S(1)}, u32[]{:S(2)}, u32[]{:S(2)}) collective-permute-start(bf16[64,1024]{1,0:T(8,128)(2,1)S(1)} %collective-permute-done.6), channel_id=1, source_target_pairs={{0,1},{1,2},{2,3},{3,4},{4,5},{5,6},{6,7},{7,8},{8,9},{9,10},{10,1... | collective-permute-start | bytes 393224 | tf_op jit(solution)/shard_map/ppermute | solution.py:20
  44.0 8.7 %collective-permute-start.9 = (bf16[64,1024]{1,0:T(8,128)(2,1)S(1)}, bf16[64,1024]{1,0:T(8,128)(2,1)S(1)}, u32[]{:S(2)}, u32[]{:S(2)}) collective-permute-start(bf16[64,1024]{1,0:T(8,128)(2,1)S(1)} %collective-permute-done.7), channel_id=1, source_target_pairs={{0,15},{1,0},{2,1},{3,2},{4,3},{5,4},{6,5},{7,6},{8,7},{9,8},{10,9... | collective-permute-start | bytes 393224 | tf_op jit(solution)/shard_map/ppermute | solution.py:25
  52.6 8.9 %collective-permute-start.10 = (bf16[64,1024]{1,0:T(8,128)(2,1)S(1)}, bf16[64,1024]{1,0:T(8,128)(2,1)S(1)}, u32[]{:S(2)}, u32[]{:S(2)}) collective-permute-start(bf16[64,1024]{1,0:T(8,128)(2,1)S(1)} %collective-permute-done.8), channel_id=1, source_target_pairs={{0,1},{1,2},{2,3},{3,4},{4,5},{5,6},{6,7},{7,8},{8,9},{9,10},{10,1... | collective-permute-start | bytes 393224 | tf_op jit(solution)/shard_map/ppermute | solution.py:20
  52.6 8.9 %collective-permute-start.11 = (bf16[64,1024]{1,0:T(8,128)(2,1)S(1)}, bf16[64,1024]{1,0:T(8,128)(2,1)S(1)}, u32[]{:S(2)}, u32[]{:S(2)}) collective-permute-start(bf16[64,1024]{1,0:T(8,128)(2,1)S(1)} %collective-permute-done.9), channel_id=1, source_target_pairs={{0,15},{1,0},{2,1},{3,2},{4,3},{5,4},{6,5},{7,6},{8,7},{9,8},{10,9... | collective-permute-start | bytes 393224 | tf_op jit(solution)/shard_map/ppermute | solution.py:25
  61.5 9.9 %collective-permute-start.12 = (bf16[64,1024]{1,0:T(8,128)(2,1)S(1)}, bf16[64,1024]{1,0:T(8,128)(2,1)S(1)}, u32[]{:S(2)}, u32[]{:S(2)}) collective-permute-start(bf16[64,1024]{1,0:T(8,128)(2,1)S(1)} %collective-permute-done.10), channel_id=1, source_target_pairs={{0,1},{1,2},{2,3},{3,4},{4,5},{5,6},{6,7},{7,8},{8,9},{9,10},{10,1... | collective-permute-start | bytes 393224 | tf_op jit(solution)/shard_map/ppermute | solution.py:20
  61.5 10.0 %collective-permute-start.13 = (bf16[64,1024]{1,0:T(8,128)(2,1)S(1)}, bf16[64,1024]{1,0:T(8,128)(2,1)S(1)}, u32[]{:S(2)}, u32[]{:S(2)}) collective-permute-start(bf16[64,1024]{1,0:T(8,128)(2,1)S(1)} %collective-permute-done.11), channel_id=1, source_target_pairs={{0,15},{1,0},{2,1},{3,2},{4,3},{5,4},{6,5},{7,6},{8,7},{9,8},{10,9... | collective-permute-start | bytes 393224 | tf_op jit(solution)/shard_map/ppermute | solution.py:25
  67.5 13.3 %copy-start.3 = (bf16[1,1,2,1024,1024]{4,3,2,1,0:T(8,128)(2,1)S(1)}, bf16[1,1,2,1024,1024]{4,3,2,1,0:T(8,128)(2,1)}, u32[]{:S(2)}) copy-start(bf16[1,1,2,1024,1024]{4,3,2,1,0:T(8,128)(2,1)} %param.6) | copy-start | bytes 12582916
  71.5 8.6 %collective-permute-start.14 = (bf16[64,1024]{1,0:T(8,128)(2,1)S(1)}, bf16[64,1024]{1,0:T(8,128)(2,1)S(1)}, u32[]{:S(2)}, u32[]{:S(2)}) collective-permute-start(bf16[64,1024]{1,0:T(8,128)(2,1)S(1)} %collective-permute-done.12), channel_id=1, source_target_pairs={{0,1},{1,2},{2,3},{3,4},{4,5},{5,6},{6,7},{7,8},{8,9},{9,10},{10,1... | collective-permute-start | bytes 393224 | tf_op jit(solution)/shard_map/ppermute | solution.py:20
  82.7 2.4 %collective-permute-start.15 = (bf16[1024,128]{1,0:T(8,128)(2,1)S(1)}, bf16[1024,128]{1,0:T(8,128)(2,1)S(1)}, u32[]{:S(2)}, u32[]{:S(2)}) collective-permute-start(bf16[1024,128]{1,0:T(8,128)(2,1)S(1)} %pad_maximum_fusion), channel_id=1, source_target_pairs={{0,16},{1,17},{2,18},{3,19},{4,20},{5,21},{6,22},{7,23},{8,24},{9,... | collective-permute-start | bytes 786440 | tf_op jit(solution)/shard_map/while/body/eval_jaxpr/ppermute | solution.py:38
  93.2 3.0 %copy-start.4 = (bf16[1,1,2,1024,1024]{4,3,2,1,0:T(8,128)(2,1)S(1)}, bf16[1,1,2,1024,1024]{4,3,2,1,0:T(8,128)(2,1)}, u32[]{:S(2)}) copy-start(bf16[1,1,2,1024,1024]{4,3,2,1,0:T(8,128)(2,1)} %param.6) | copy-start | bytes 12582916
Sparse Core Ops, SparseCore 0:
  93.4 91.3 reduce-scatter.3
